TPU v7x, 128 devices: a whole 4x4x4 slice. The times are simulated.
128 devices in a mesh: group: 4 (over y_lo, core), mp: 32 (over z, x, y_hi).
Axes of the slice: x: 4, y: 4 (y_hi: 2, y_lo: 2; y = y_hi * 2 + y_lo), z: 4, core: 2. Of those that a mesh axis runs over, the one named last changes fastest.
Arguments:
- tokens: bfloat16 [5120, 2048], P(('group', 'mp')), may hold values from -6 to 6
- lengths: int32 [4, 8], P('group'), may hold values from 1 to 512, 1280 in all within a row
- query_gain: float32 [2048], replicated, may hold values from 0.5 to 8
- key_gain: float32 [2048], replicated, may hold values from 0.5 to 8
- attn_post_gain: float32 [2048], replicated, may hold values from 0.5 to 1.5
- mlp_post_gain: float32 [2048], replicated, may hold values from 0.5 to 1.5
- query_weight: float32 [2048, 2048], P(('mp', 'group')), may hold values from -4 to 4
- key_weight: float32 [2048, 2048], P(('mp', 'group')), may hold values from -4 to 4
- value_weight: float32 [2048, 2048], P(('mp', 'group')), may hold values from -0.125 to 0.125
- output_weight: float32 [2048, 2048], P(('mp', 'group')), may hold values from -0.125 to 0.125
- gate_weight: float32 [2048, 8192], P(('mp', 'group')), may hold values from -0.125 to 0.125
- up_weight: float32 [2048, 8192], P(('mp', 'group')), may hold values from -0.125 to 0.125
- down_weight: float32 [8192, 2048], P(('mp', 'group')), may hold values from -0.0625 to 0.0625
Outputs:
- layer_out: bfloat16 [5120, 2048], P(('group', 'mp'))
Inputs may be any that keep to these rules, and one draw needn't show every extreme that they name: In each group the 8 prompt lengths sum to 1280; the longest is exactly 512.
All inputs are finite; a program needn't handle non-finite values.
Results may differ from a plain program's by a relative error of at most 0.034.
Values may be sent and summed in bfloat16 or wider, within the bound.
A program may use at most 64 MiB of HBM per device.

v0:
```python
import math
import jax
import jax.numpy as jnp
from jax import lax
from jax.sharding import Mesh, PartitionSpec as P

HEAD_DIM = 128
NORM_EPSILON = 1e-06
ROPE_BASE = 500000.0
PLANE = ("z", "x")
COLUMN = ("yhi", "ylo", "core")


def segments(prompt_lens, rows):
    seg_ends = jnp.cumsum(prompt_lens)
    starts = seg_ends - prompt_lens
    segment = jnp.sum((rows[:, None] >= seg_ends[None, :]).astype(jnp.int32), axis=1)
    member = segment[:, None] == jnp.arange(prompt_lens.shape[0], dtype=jnp.int32)[None, :]
    opening = jnp.sum(jnp.where(member, starts[None, :], 0), axis=1)
    return (segment, rows - opening)


def rotary(values_in, cosines, sines):
    half = HEAD_DIM // 2
    front, back = (values_in[:, :half], values_in[:, half:])
    return jnp.concatenate(
        [front * cosines - back * sines, back * cosines + front * sines], axis=-1
    )


def rms_scale(values_in, gain):
    return (
        values_in
        * lax.rsqrt(jnp.mean(values_in * values_in, axis=-1, keepdims=True) + NORM_EPSILON)
        * gain
    )


def sum_scatter(partial, tok_rows):
    blocks = partial.astype(jnp.bfloat16).reshape(-1, tok_rows, partial.shape[1])
    got = lax.all_to_all(blocks, PLANE, split_axis=0, concat_axis=0, tiled=True)
    return jnp.sum(got.astype(jnp.float32), axis=0)


def column_blocks(weights, parts):
    rows = weights[0].shape[0]
    split = [w.astype(jnp.bfloat16).reshape(rows, parts, -1) for w in weights]
    blocks = jnp.concatenate(split, axis=2).transpose(1, 0, 2)
    got = lax.all_to_all(blocks, PLANE, split_axis=0, concat_axis=0, tiled=True)
    whole = lax.all_gather(got, COLUMN, axis=1, tiled=True)
    return whole.reshape(-1, whole.shape[2])


def row_blocks(weight):
    return lax.all_gather(weight.astype(jnp.bfloat16), COLUMN, axis=0, tiled=True)


def per_device(
    tokens,
    lengths,
    query_gain,
    key_gain,
    attn_post_gain,
    mlp_post_gain,
    query_weight,
    key_weight,
    value_weight,
    output_weight,
    gate_weight,
    up_weight,
    down_weight,
):
    features = tokens.shape[1]
    parts = lax.axis_size("z") * lax.axis_size("x")
    place = lax.axis_index("z") * lax.axis_size("x") + lax.axis_index("x")
    half = lax.axis_index("yhi")
    tok_rows = tokens.shape[0]
    set_rows = tok_rows * parts
    qkv = column_blocks([query_weight, key_weight, value_weight], parts)
    output_block = row_blocks(output_weight)
    mlp_weights = column_blocks([gate_weight, up_weight], parts)
    down_block = row_blocks(down_weight)
    gathered = lax.all_gather(tokens, PLANE, axis=0, tiled=True)
    projected = jnp.dot(gathered, qkv, preferred_element_type=jnp.float32)
    q_raw, k_raw, v_raw = jnp.split(projected, 3, axis=1)
    squares = jnp.stack([jnp.sum(q_raw * q_raw, axis=1), jnp.sum(k_raw * k_raw, axis=1)])
    totals = jnp.sum(lax.all_gather(squares, PLANE, axis=0, tiled=False), axis=0)
    q_part = lax.dynamic_slice_in_dim(query_gain, place * HEAD_DIM, HEAD_DIM)
    k_part = lax.dynamic_slice_in_dim(key_gain, place * HEAD_DIM, HEAD_DIM)
    q_normed = q_raw * lax.rsqrt(totals[0] / features + NORM_EPSILON)[:, None] * q_part
    k_normed = k_raw * lax.rsqrt(totals[1] / features + NORM_EPSILON)[:, None] * k_part
    index = jnp.arange(set_rows, dtype=jnp.int32)

    def rows_of(which):
        return (index // tok_rows * 2 + which) * tok_rows + index % tok_rows

    my_rows = rows_of(half)
    segment, position = segments(lengths[0], my_rows)
    frequency = jnp.exp(
        jnp.arange(HEAD_DIM // 2, dtype=jnp.float32) * (-2.0 * math.log(ROPE_BASE) / HEAD_DIM)
    )
    angles = position.astype(jnp.float32)[:, None] * frequency[None, :]
    cosines, sines = (jnp.cos(angles), jnp.sin(angles))
    queries = rotary(q_normed, cosines, sines).astype(jnp.bfloat16)
    keys_rot = rotary(k_normed, cosines, sines).astype(jnp.bfloat16)
    kv_mine = jnp.concatenate([keys_rot, v_raw.astype(jnp.bfloat16)], axis=1)
    kv_other = lax.ppermute(kv_mine, "yhi", [(0, 1), (1, 0)])
    kv = jnp.concatenate([kv_mine, kv_other], axis=0)
    key_rows = jnp.concatenate([my_rows, rows_of(1 - half)])
    key_segment, _ = segments(lengths[0], key_rows)
    scores = lax.dot_general(
        queries, kv[:, :HEAD_DIM], (((1,), (1,)), ((), ())), preferred_element_type=jnp.float32
    ) * (1.0 / math.sqrt(HEAD_DIM))
    allowed = (segment[:, None] == key_segment[None, :]) & (key_rows[None, :] <= my_rows[:, None])
    scores = jnp.where(allowed, scores, -1e30)
    weights = jnp.exp(scores - jnp.max(scores, axis=1, keepdims=True))
    weights = weights / jnp.sum(weights, axis=1, keepdims=True)
    attended = jnp.dot(
        weights.astype(jnp.bfloat16), kv[:, HEAD_DIM:], preferred_element_type=jnp.float32
    ).astype(jnp.bfloat16)
    attn_out = sum_scatter(
        jnp.dot(attended, output_block, preferred_element_type=jnp.float32), tok_rows
    )
    hidden = (tokens.astype(jnp.float32) + rms_scale(attn_out, attn_post_gain)).astype(jnp.bfloat16)
    both_proj = jnp.dot(
        lax.all_gather(hidden, PLANE, axis=0, tiled=True),
        mlp_weights,
        preferred_element_type=jnp.float32,
    )
    width = both_proj.shape[1] // 2
    activated = (jax.nn.silu(both_proj[:, :width]) * both_proj[:, width:]).astype(jnp.bfloat16)
    mlp_out = sum_scatter(
        jnp.dot(activated, down_block, preferred_element_type=jnp.float32), tok_rows
    )
    return (hidden.astype(jnp.float32) + rms_scale(mlp_out, mlp_post_gain)).astype(jnp.bfloat16)


def solution(mesh):
    fine = Mesh(mesh.devices.reshape(2, 2, 4, 4, 2), ("ylo", "core", "z", "x", "yhi"))
    tok = P(("ylo", "core", "z", "x", "yhi"), None)
    weight = P(("z", "x", "yhi", "ylo", "core"), None)
    return jax.shard_map(
        per_device,
        mesh=fine,
        in_specs=(tok, P(("ylo", "core"), None), P(), P(), P(), P()) + (weight,) * 7,
        out_specs=tok,
        check_vma=False,
    )
```

profile of v0, /device:TPU:0, one launch (start us, length us, event | category | flops | bytes accessed | tf_op | source)
XLA Modules:
  0.0 315.3 jit_solution(8745225860466606189)
XLA Ops:
  6.5 0.0 all-gather.8.cloned.1.call-start
  6.5 1.0 convert_bitcast_fusion.2
  7.6 0.9 convert_bitcast_fusion.1
  8.5 0.9 convert_bitcast_fusion
  9.5 16.1 %all_to_all.20 = bf16[16,16,384]{2,1,0:T(8,128)(2,1)S(1)} all-to-all(bf16[16,16,384]{2,1,0:T(8,128)(2,1)S(1)} %copy.22), channel_id=1, replica_groups=mesh['ylo'=2,'core'=2,'z'=4,'x'=4,'yhi'=2] {'z','x'}, dimensions={0} | all-to-all | bytes 393216 | tf_op jit(solution)/shard_map/all_to_all | solution.py:49
  25.6 0.7 copy.23
  26.4 0.0 all-gather.8.cloned.1.call-update
  26.4 0.0 all-gather.10.cloned.1.call-start
  26.4 0.7 all-gather.10.cloned.1.call-update
  27.2 0.1 copy.31
  27.3 0.0 copy-done.4
  27.3 0.0 copy-start.9
  27.3 0.0 copy-start.6
  27.3 0.1 copy.32
  27.4 0.1 maximum_bitcast_fusion
  27.5 1.1 copy.25
  28.6 3.6 %all-to-all-start.2 = ((bf16[16,16,1024]{2,1,0:T(8,128)(2,1)}), bf16[16,16,1024]{2,1,0:T(8,128)(2,1)S(1)}, u32[]{:S(2)}, u32[]{:S(2)}) async-start(bf16[16,16,1024]{2,1,0:T(8,128)(2,1)} %copy.25), calls=%async_computation.2 | async-start | bytes 1048576 | tf_op jit(solution)/shard_map/all_to_all | solution.py:49
  32.2 0.0 all-gather.14.cloned.1.call-start
  32.3 10.3 %all-to-all-done.2 = bf16[16,16,1024]{2,1,0:T(8,128)(2,1)S(1)} async-done(((bf16[16,16,1024]{2,1,0:T(8,128)(2,1)}), bf16[16,16,1024]{2,1,0:T(8,128)(2,1)S(1)}, u32[]{:S(2)}, u32[]{:S(2)}) %all-to-all-start.2) | async-done | bytes 524320 | tf_op jit(solution)/shard_map/all_to_all | solution.py:49
  42.6 1.1 copy.26
  43.7 0.0 all-gather.14.cloned.1.call-update
  43.7 0.0 all-gather.12.cloned.1.call-start
  43.8 0.8 dynamic_slice.6
  44.6 0.8 dynamic_slice.7
  45.3 0.2 reduce-window.4
  45.5 0.0 copy-done.6
  45.5 0.1 convert_reduce_fusion.3
  45.6 0.1 select_reduce_fusion
  45.7 3.0 all-gather.8.cloned.1.call-done
  48.7 1.8 copy.24
  50.5 46.8 %all-gather.10.cloned.1.call-done = bf16[640,2048]{1,0:T(8,128)(2,1)} async-done(((bf16[40,2048]{1,0:T(8,128)(2,1)}), bf16[640,2048]{1,0:T(8,128)(2,1)}) %all-gather.10.cloned.1.call-update) | async-done | bytes 2621456 | tf_op jit(solution)/shard_map/all_gather | solution.py:83
  97.3 3.2 %convolution_bitcast_fusion = f32[640,384]{0,1:T(8,128)S(1)} fusion(bf16[2048,384]{1,0:T(8,128)(2,1)S(1)} %bitcast.42, bf16[640,2048]{1,0:T(8,128)(2,1)} %all-gather.10.cloned.1.call-done), kind=kOutput, calls=%fused_computation.10 | convolution fusion | flops 1006632960 | bytes 5177344 | tf_op jit(solution)/shard_map/dot_general | solution.py:84
  100.5 0.1 multiply_reduce_fusion.3
  100.6 22.9 %all-gather.1 = f32[16,2,640]{2,1,0:T(2,128)S(1)} all-gather(f32[1,2,640]{2,1,0:T(2,128)S(1)} %maximum_bitcast_fusion.2), channel_id=2, replica_groups=mesh['ylo'=2,'core'=2,'z'=4,'x'=4,'yhi'=2] {'z','x'}, dimensions={0}, use_global_device_ids=true | all-gather | bytes 87040 | tf_op jit(solution)/shard_map/all_gather | solution.py:87
  123.6 0.1 multiply_multiply_fusion.1
  123.7 0.7 fusion.19
  124.5 3.1 collective-permute-start
  127.6 0.1 convert_reduce_fusion.2
  127.7 17.3 %all_gather.28 = bf16[128,2048]{1,0:T(8,128)(2,1)} all-gather(bf16[16,2048]{1,0:T(8,128)(2,1)S(1)} %convert_element_type.79), channel_id=1, replica_groups=mesh['ylo'=2,'core'=2,'z'=4,'x'=4,'yhi'=2] {'yhi','ylo','core'}, dimensions={0}, use_global_device_ids=true | all-gather | bytes 589824 | tf_op jit(solution)/shard_map/all_gather | solution.py:55
  145.0 0.0 collective-permute-done
  145.1 1.0 fusion.48
  146.1 0.6 fusion.1
  146.7 4.9 %convolution_convert_fusion.1 = bf16[640,2048]{1,0:T(8,128)(2,1)} fusion(bf16[128,2048]{1,0:T(8,128)(2,1)} %all_gather.28, f32[640,1280]{1,0:T(8,128)S(1)} %get-tuple-element.18, f32[640]{0:T(1024)S(1)} %fusion.1, f32[640]{0:T(1024)S(1)} %get-tuple-element.17, bf16[1280,256]{0,1:T(8,128)(2,1)} %copy-done.1), kind=kOutput, calls=%fused_computation.7 | convolution fusion | flops 549109760 | bytes 6755328 | tf_op jit(solution)/shard_map/dot_general | solution.py:122
  151.6 40.8 %all_to_all.21 = bf16[16,40,2048]{2,1,0:T(8,128)(2,1)S(1)} all-to-all(bf16[16,40,2048]{2,1,0:T(8,128)(2,1)} %bitcast.40), channel_id=1, replica_groups=mesh['ylo'=2,'core'=2,'z'=4,'x'=4,'yhi'=2] {'z','x'}, dimensions={0} | all-to-all | bytes 5242880 | tf_op jit(solution)/shard_map/all_to_all | solution.py:41
  192.4 0.5 convert_reduce_fusion.1
  192.9 0.1 multiply_reduce_fusion.1
  193.0 0.3 copy-done.2
  193.3 0.8 add_convert_fusion.1
  194.1 0.0 all-gather.12.cloned.1.call-update
  194.1 0.2 all-gather.16.cloned.1.call-start
  194.4 0.7 convert_element_type.87
  195.1 0.0 all-gather.16.cloned.1.call-update
  195.1 0.0 all-gather.14.cloned.1.call-done
  195.1 6.5 %copy.27 = bf16[16,128,1024]{2,1,0:T(8,128)(2,1)} copy(bf16[16,128,1024]{2,0,1:T(8,128)(2,1)} %all-gather.14.cloned.1.call-done) | data formatting | bytes 8388608 | tf_op jit(solution)/shard_map/all_gather | solution.py:50
  201.6 35.2 %all-gather.12.cloned.1.call-done = bf16[640,2048]{1,0:T(8,128)(2,1)} async-done(((bf16[40,2048]{1,0:T(8,128)(2,1)}), bf16[640,2048]{1,0:T(8,128)(2,1)}) %all-gather.12.cloned.1.call-update) | async-done | bytes 2621456 | tf_op jit(solution)/shard_map/all_gather | solution.py:126
  236.8 5.4 %fusion.49 = f32[640,1024]{1,0:T(8,128)S(1)} fusion(bf16[640,2048]{1,0:T(8,128)(2,1)} %all-gather.12.cloned.1.call-done, bf16[2048,1024]{1,0:T(8,128)(2,1)} %bitcast.39), kind=kOutput, calls=%fused_computation.91 | convolution fusion | flops 2684354560 | bytes 9437184 | tf_op jit(solution)/shard_map/dot_general | solution.py:125
  242.2 20.6 %all-gather.16.cloned.1.call-done = bf16[512,2048]{1,0:T(8,128)(2,1)} async-done(((bf16[64,2048]{1,0:T(8,128)(2,1)}), bf16[512,2048]{1,0:T(8,128)(2,1)}) %all-gather.16.cloned.1.call-update) | async-done | bytes 2097168 | tf_op jit(solution)/shard_map/all_gather | solution.py:55
  262.8 3.1 convolution_convert_fusion
  265.9 41.2 %all_to_all.22 = bf16[16,40,2048]{2,1,0:T(8,128)(2,1)S(1)} all-to-all(bf16[16,40,2048]{2,1,0:T(8,128)(2,1)S(1)} %bitcast.41), channel_id=1, replica_groups=mesh['ylo'=2,'core'=2,'z'=4,'x'=4,'yhi'=2] {'z','x'}, dimensions={0} | all-to-all | bytes 5242880 | tf_op jit(solution)/shard_map/all_to_all | solution.py:41
  307.1 0.5 convert_reduce_fusion
  307.6 0.1 multiply_reduce_fusion
  307.8 0.3 copy-done
  308.0 0.0 copy-done.8
  308.0 0.8 add_convert_fusion
  (37 shorter events, 0.5 us)
Async XLA Ops:
  6.5 20.6 %copy-start.3 = (f32[16,8192]{1,0:T(8,128)S(1)}, f32[16,8192]{1,0:T(8,128)}, u32[]{:S(2)}) copy-start(f32[16,8192]{1,0:T(8,128)} %param.23) | copy-start | bytes 1572868
  6.5 20.7 %copy-start.4 = (f32[16,8192]{1,0:T(8,128)S(1)}, f32[16,8192]{1,0:T(8,128)}, u32[]{:S(2)}) copy-start(f32[16,8192]{1,0:T(8,128)} %param.24) | copy-start | bytes 1572868
  6.5 42.2 %all-gather.8.cloned.1.call-start = ((), (), s32[]{:S(2)}) async-start(), calls=%async_computation.4 | async-start | bytes 1769472 | tf_op jit(solution)/shard_map/all_gather | solution.py:50
  26.4 70.9 %all-gather.10.cloned.1.call-start = ((), (), s32[]{:S(2)}) async-start(), calls=%async_computation.5 | async-start | bytes 2785280 | tf_op jit(solution)/shard_map/all_gather | solution.py:83
  27.3 18.0 %copy-start.9 = (s32[1,8]{1,0:T(1,128)S(1)}, s32[1,8]{1,0:T(1,128)}, u32[]{:S(2)}) copy-start(s32[1,8]{1,0:T(1,128)} %param.14) | copy-start | bytes 100
  27.3 18.2 %copy-start.6 = (f32[16,2048]{1,0:T(8,128)S(1)}, f32[16,2048]{1,0:T(8,128)}, u32[]{:S(2)}) copy-start(f32[16,2048]{1,0:T(8,128)} %param.22) | copy-start | bytes 393220
  28.6 14.0 %all-to-all-start.2 = ((bf16[16,16,1024]{2,1,0:T(8,128)(2,1)}), bf16[16,16,1024]{2,1,0:T(8,128)(2,1)S(1)}, u32[]{:S(2)}, u32[]{:S(2)}) async-start(bf16[16,16,1024]{2,1,0:T(8,128)(2,1)} %copy.25), calls=%async_computation.2 | async-start | bytes 1048576 | tf_op jit(solution)/shard_map/all_to_all | solution.py:49
  32.2 163.0 %all-gather.14.cloned.1.call-start = ((), (), s32[]{:S(2)}) async-start(), calls=%async_computation.7 | async-start | bytes 4718592 | tf_op jit(solution)/shard_map/all_gather | solution.py:50
  43.7 193.1 %all-gather.12.cloned.1.call-start = ((), (), s32[]{:S(2)}) async-start(), calls=%async_computation.6 | async-start | bytes 2785280 | tf_op jit(solution)/shard_map/all_gather | solution.py:126
  124.5 20.5 %collective-permute-start = (bf16[640,256]{0,1:T(8,128)(2,1)S(1)}, bf16[640,256]{0,1:T(8,128)(2,1)S(1)}, u32[]{:S(2)}, u32[]{:S(2)}) collective-permute-start(bf16[640,256]{0,1:T(8,128)(2,1)S(1)} %pad_maximum_fusion.1), channel_id=1, source_target_pairs={{0,1},{1,0},{2,3},{3,2},{4,5},{5,4},{6,7},{7,6},{8,9},{9,8},{10,11... | collective-permute-start | bytes 983048 | tf_op jit(solution)/shard_map/ppermute | solution.py:107
  145.1 1.1 copy-start.1
  192.4 0.9 copy-start.2
  192.4 0.9 copy-start.7
  192.4 2.0 copy-start.5
  194.1 68.7 %all-gather.16.cloned.1.call-start = ((), (), s32[]{:S(2)}) async-start(), calls=%async_computation.8 | async-start | bytes 2359296 | tf_op jit(solution)/shard_map/all_gather | solution.py:55
  307.1 0.9 copy-start
  307.1 0.9 copy-start.8
Sparse Core Ops, SparseCore 0:
  26.5 22.1 all-gather.7
  50.9 46.3 all-gather.9
  99.0 36.7 all-gather.13
  194.2 42.4 all-gather.11
  238.3 24.4 all-gather.15
where the time goes:
time: 316 us; the launch traced here: 315 us
  blocking collectives  138 us (44%)
  waiting for transfers between devices  117 us (37%)
  matrix products  17.6 us (6%)
  local copies, waits for them, and re-layouts  13.6 us (4%)
  between operations  13.5 us (4%)
  other arithmetic  8.72 us (3%)
  starting transfers between devices  7.01 us (2%)
    all_to_all x2, blocking collectives, sum_scatter(): got = lax.all_to_all(blocks, PLANE, split_axis=0, concat_axis=0, tiled=True)  82 us
    all_gather x1, waiting for transfers between devices, per_device(): gathered = lax.all_gather(tokens, PLANE, axis=0, tiled=True)  46.8 us
    all_gather x1, waiting for transfers between devices, per_device(): lax.all_gather(hidden, PLANE, axis=0, tiled=True)  35.2 us
    all_gather x1, blocking collectives, per_device(): lax.all_gather(squares, PLANE, axis=0, tiled=False)  22.9 us
    all_gather x1, waiting for transfers between devices, row_blocks(): lax.all_gather(weight.astype(jnp.bfloat16), COLUMN, axis=0, tiled=True)  20.6 us
    all_gather x1, blocking collectives, row_blocks(): lax.all_gather(weight.astype(jnp.bfloat16), COLUMN, axis=0, tiled=True)  17.3 us
    all_to_all x1, blocking collectives, column_blocks(): got = lax.all_to_all(blocks, PLANE, split_axis=0, concat_axis=0, tiled=True)  16.1 us
    all_to_all x1, waiting for transfers between devices, column_blocks(): got = lax.all_to_all(blocks, PLANE, split_axis=0, concat_axis=0, tiled=True)  10.3 us
  transfers between devices with their start and end apart: 7, of which 5 were waited for; matrix products, arithmetic and copies ran while one was open for 10% of the time, Pallas kernels for 0%

commit v1 on v0

--- a/solution.py
+++ b/solution.py
@@ -9,6 +9,11 @@
 ROPE_BASE = 500000.0
 PLANE = ("z", "x")
 COLUMN = ("yhi", "ylo", "core")
+
+
+def exchange_gather(x, axis, along):
+    sent = jnp.stack([x] * lax.axis_size(axis))
+    return jnp.concatenate(lax.all_to_all(sent, axis, 0, 0), axis=along)
 
 
 def segments(prompt_lens, rows):
@@ -47,7 +52,7 @@
     split = [w.astype(jnp.bfloat16).reshape(rows, parts, -1) for w in weights]
     blocks = jnp.concatenate(split, axis=2).transpose(1, 0, 2)
     got = lax.all_to_all(blocks, PLANE, split_axis=0, concat_axis=0, tiled=True)
-    whole = lax.all_gather(got, COLUMN, axis=1, tiled=True)
+    whole = exchange_gather(got, COLUMN, 1)
     return whole.reshape(-1, whole.shape[2])
 
 

time: 316 us -> 291 us (0.921)
  waiting for transfers between devices: 117 us -> 82.7 us
  blocking collectives: 138 us -> 145 us
  starting transfers between devices: 7.01 us -> 12.5 us
    all_to_all x1 -> x2, waiting for transfers between devices: 10.3 us -> 76.6 us  [exchange_gather(): return jnp.concatenate(lax.all_to_all(sent, axis, 0, 0), axis=along)]
    all_gather x1, waiting for transfers between devices: 46.8 us -> 5.35 us  [per_device(): gathered = lax.all_gather(tokens, PLANE, axis=0, tiled=True)]
    all_gather x1, waiting for transfers between devices: 35.2 us -> 0.01 us  [per_device(): lax.all_gather(hidden, PLANE, axis=0, tiled=True)]
    all_gather x1, waiting for transfers between devices: 20.6 us -> 0.02 us  [row_blocks(): lax.all_gather(weight.astype(jnp.bfloat16), COLUMN, axis=0, tiled=True)]
    all_to_all x1 -> x2, blocking collectives: 16.1 us -> 31.1 us  [column_blocks(): got = lax.all_to_all(blocks, PLANE, split_axis=0, concat_axis=0, tiled=True)]
    all_gather x2 -> x0, local copies, waits for them, and re-layouts: 8.25 us -> none  [column_blocks(): whole = lax.all_gather(got, COLUMN, axis=1, tiled=True)]
    all_to_all x2, blocking collectives: 82 us -> 75.3 us  [sum_scatter(): got = lax.all_to_all(blocks, PLANE, split_axis=0, concat_axis=0, tiled=True)]
    all_to_all x1 -> x2, starting transfers between devices: 3.57 us -> 9.15 us  [exchange_gather(): return jnp.concatenate(lax.all_to_all(sent, axis, 0, 0), axis=along)]
  transfers between devices with their start and end apart: 7 -> 6, of which waited for: 5 -> 3; matrix products, arithmetic and copies ran while one was open for 10% -> 7% of each run, Pallas kernels for 0% -> 0%
where the time goes in v1:
time: 291 us; the launch traced here: 290 us
  blocking collectives  145 us (50%)
  waiting for transfers between devices  82.7 us (28%)
  matrix products  17.6 us (6%)
  between operations  13.4 us (5%)
  starting transfers between devices  12.5 us (4%)
  local copies, waits for them, and re-layouts  11.2 us (4%)
  other arithmetic  7.82 us (3%)
    all_to_all x2, waiting for transfers between devices, exchange_gather(): return jnp.concatenate(lax.all_to_all(sent, axis, 0, 0), axis=along)  76.6 us
    all_to_all x2, blocking collectives, sum_scatter(): got = lax.all_to_all(blocks, PLANE, split_axis=0, concat_axis=0, tiled=True)  75.3 us
    all_to_all x2, blocking collectives, column_blocks(): got = lax.all_to_all(blocks, PLANE, split_axis=0, concat_axis=0, tiled=True)  31.1 us
    all_gather x1, blocking collectives, per_device(): lax.all_gather(squares, PLANE, axis=0, tiled=False)  23 us
    all_gather x1, blocking collectives, row_blocks(): lax.all_gather(weight.astype(jnp.bfloat16), COLUMN, axis=0, tiled=True)  15.2 us
    all_to_all x2, starting transfers between devices, exchange_gather(): return jnp.concatenate(lax.all_to_all(sent, axis, 0, 0), axis=along)  9.15 us
  transfers between devices with their start and end apart: 6, of which 3 were waited for; matrix products, arithmetic and copies ran while one was open for 7% of the time, Pallas kernels for 0%

profile of v1, /device:TPU:0, one launch (start us, length us, event | category | flops | bytes accessed | tf_op | source)
XLA Modules:
  0.0 289.8 jit_solution(13893176333669941131)
XLA Ops:
  6.5 0.0 all-gather.6.cloned.1.call-start
  6.5 0.7 all-gather.6.cloned.1.call-update
  7.3 0.9 copy_bitcast_fusion.4
  8.2 1.0 copy_bitcast_fusion.2
  9.2 0.0 copy-start.9
  9.2 0.0 copy-start.6
  9.2 16.2 %all_to_all.30 = bf16[16,16,384]{2,1,0:T(8,128)(2,1)S(1)} all-to-all(bf16[16,16,384]{2,1,0:T(8,128)(2,1)S(1)} %maximum_bitcast_fusion.1), channel_id=1, replica_groups=mesh['ylo'=2,'core'=2,'z'=4,'x'=4,'yhi'=2] {'z','x'}, dimensions={0} | all-to-all | bytes 393216 | tf_op jit(solution)/shard_map/all_to_all | solution.py:54
  25.5 1.3 stack.10
  26.7 4.5 %all-to-all-start.1 = ((bf16[8,16,16,384]{3,2,1,0:T(8,128)(2,1)}), bf16[8,16,16,384]{3,2,1,0:T(8,128)(2,1)S(1)}, u32[]{:S(2)}, u32[]{:S(2)}) async-start(bf16[8,16,16,384]{3,2,1,0:T(8,128)(2,1)} %stack.10), calls=%async_computation.1 | async-start | bytes 3145728 | tf_op jit(solution)/shard_map/all_to_all | solution.py:16
  31.2 0.0 all-gather.8.cloned.1.call-start
  31.3 0.8 dynamic_slice.6
  32.0 0.8 dynamic_slice.7
  32.8 0.0 copy-done.9
  32.8 0.2 reduce-window.4
  33.0 0.0 copy-done.6
  33.1 0.1 convert_reduce_fusion.3
  33.2 0.1 select_reduce_fusion
  33.3 19.5 %all-to-all-done.1 = bf16[8,16,16,384]{3,2,1,0:T(8,128)(2,1)S(1)} async-done(((bf16[8,16,16,384]{3,2,1,0:T(8,128)(2,1)}), bf16[8,16,16,384]{3,2,1,0:T(8,128)(2,1)S(1)}, u32[]{:S(2)}, u32[]{:S(2)}) %all-to-all-start.1) | async-done | bytes 1572896 | tf_op jit(solution)/shard_map/all_to_all | solution.py:16
  52.8 0.2 copy.31
  53.0 5.3 %all-gather.6.cloned.1.call-done = bf16[640,2048]{1,0:T(8,128)(2,1)} async-done(((bf16[40,2048]{1,0:T(8,128)(2,1)}), bf16[640,2048]{1,0:T(8,128)(2,1)}) %all-gather.6.cloned.1.call-update) | async-done | bytes 2621456 | tf_op jit(solution)/shard_map/all_gather | solution.py:88
  58.4 3.2 %convolution_bitcast_fusion = f32[640,384]{0,1:T(8,128)S(1)} fusion(bf16[2048,384]{1,0:T(8,128)(2,1)S(1)} %bitcast.54, bf16[640,2048]{1,0:T(8,128)(2,1)} %all-gather.6.cloned.1.call-done), kind=kOutput, calls=%fused_computation.10 | convolution fusion | flops 1006632960 | bytes 5177344 | tf_op jit(solution)/shard_map/dot_general | solution.py:89
  61.5 0.1 multiply_reduce_fusion.3
  61.7 23.0 %all-gather.1 = f32[16,2,640]{2,1,0:T(2,128)S(1)} all-gather(f32[1,2,640]{2,1,0:T(2,128)S(1)} %maximum_bitcast_fusion.2), channel_id=2, replica_groups=mesh['ylo'=2,'core'=2,'z'=4,'x'=4,'yhi'=2] {'z','x'}, dimensions={0}, use_global_device_ids=true | all-gather | bytes 87040 | tf_op jit(solution)/shard_map/all_gather | solution.py:92
  84.7 0.1 multiply_multiply_fusion.1
  84.8 0.7 fusion.19
  85.6 3.1 %collective-permute-start = (bf16[640,256]{0,1:T(8,128)(2,1)S(1)}, bf16[640,256]{0,1:T(8,128)(2,1)S(1)}, u32[]{:S(2)}, u32[]{:S(2)}) collective-permute-start(bf16[640,256]{0,1:T(8,128)(2,1)S(1)} %pad_maximum_fusion.1), channel_id=1, source_target_pairs={{0,1},{1,0},{2,3},{3,2},{4,5},{5,4},{6,7},{7,6},{8,9},{9,8},{10,11... | collective-permute-start | bytes 983048 | tf_op jit(solution)/shard_map/ppermute | solution.py:112
  88.7 0.1 convert_reduce_fusion.2
  88.8 15.2 %all_gather.21 = bf16[128,2048]{1,0:T(8,128)(2,1)} all-gather(bf16[16,2048]{1,0:T(8,128)(2,1)S(1)} %convert_element_type.79), channel_id=1, replica_groups=mesh['ylo'=2,'core'=2,'z'=4,'x'=4,'yhi'=2] {'yhi','ylo','core'}, dimensions={0}, use_global_device_ids=true | all-gather | bytes 589824 | tf_op jit(solution)/shard_map/all_gather | solution.py:60
  104.0 0.0 collective-permute-done
  104.1 0.0 copy-start.1
  104.1 1.1 fusion.48
  105.1 0.0 copy-done.1
  105.1 0.6 fusion.1
  105.7 4.8 %convolution_convert_fusion.1 = bf16[640,2048]{1,0:T(8,128)(2,1)} fusion(bf16[128,2048]{1,0:T(8,128)(2,1)} %all_gather.21, f32[640,1280]{1,0:T(8,128)S(1)} %get-tuple-element.18, f32[640]{0:T(1024)S(1)} %fusion.1, f32[640]{0:T(1024)S(1)} %get-tuple-element.17, bf16[1280,256]{0,1:T(8,128)(2,1)} %copy-done.1), kind=kOutput, calls=%fused_computation.7 | convolution fusion | flops 549109760 | bytes 6755328 | tf_op jit(solution)/shard_map/dot_general | solution.py:127
  110.6 38.6 %all_to_all.31 = bf16[16,40,2048]{2,1,0:T(8,128)(2,1)S(1)} all-to-all(bf16[16,40,2048]{2,1,0:T(8,128)(2,1)} %bitcast.52), channel_id=1, replica_groups=mesh['ylo'=2,'core'=2,'z'=4,'x'=4,'yhi'=2] {'z','x'}, dimensions={0} | all-to-all | bytes 5242880 | tf_op jit(solution)/shard_map/all_to_all | solution.py:46
  149.1 0.0 copy-start.2
  149.2 0.5 convert_reduce_fusion.1
  149.7 0.1 multiply_reduce_fusion.1
  149.8 0.3 copy-done.2
  150.1 0.0 copy-done.7
  150.1 0.8 add_convert_fusion.1
  150.9 0.0 all-gather.8.cloned.1.call-update
  150.9 0.0 copy-done.3
  150.9 0.0 copy-done.4
  151.0 0.1 copy_bitcast_fusion
  151.0 0.1 maximum_bitcast_fusion
  151.1 14.9 %all_to_all.32 = bf16[16,16,1024]{2,1,0:T(8,128)(2,1)S(1)} all-to-all(bf16[16,16,1024]{2,1,0:T(8,128)(2,1)S(1)} %maximum_bitcast_fusion), channel_id=1, replica_groups=mesh['ylo'=2,'core'=2,'z'=4,'x'=4,'yhi'=2] {'z','x'}, dimensions={0} | all-to-all | bytes 1048576 | tf_op jit(solution)/shard_map/all_to_all | solution.py:54
  165.9 2.5 stack.14
  168.5 4.7 %all-to-all-start.4 = ((bf16[8,16,16,1024]{3,2,1,0:T(8,128)(2,1)}), bf16[8,16,16,1024]{3,2,1,0:T(8,128)(2,1)}, u32[]{:S(2)}, u32[]{:S(2)}) async-start(bf16[8,16,16,1024]{3,2,1,0:T(8,128)(2,1)} %stack.14), calls=%async_computation.4 | async-start | bytes 8388608 | tf_op jit(solution)/shard_map/all_to_all | solution.py:16
  173.1 0.2 all-gather.10.cloned.1.call-start
  173.4 0.0 copy-done.5
  173.4 0.7 convert_element_type.87
  174.1 0.0 all-gather.10.cloned.1.call-update
  174.2 57.1 %all-to-all-done.4 = bf16[8,16,16,1024]{3,2,1,0:T(8,128)(2,1)} async-done(((bf16[8,16,16,1024]{3,2,1,0:T(8,128)(2,1)}), bf16[8,16,16,1024]{3,2,1,0:T(8,128)(2,1)}, u32[]{:S(2)}, u32[]{:S(2)}) %all-to-all-start.4) | async-done | bytes 4194336 | tf_op jit(solution)/shard_map/all_to_all | solution.py:16
  231.2 5.0 %copy.34 = bf16[8,16,16,1024]{3,2,0,1:T(8,128)(2,1)} copy(bf16[8,16,16,1024]{3,2,1,0:T(8,128)(2,1)} %all-to-all-done.4) | data formatting | bytes 8388608 | tf_op jit(solution)/shard_map/all_to_all | solution.py:16
  236.2 5.4 %fusion.49 = f32[640,1024]{1,0:T(8,128)S(1)} fusion(bf16[640,2048]{1,0:T(8,128)(2,1)} %all-gather.8.cloned.1.call-done, bf16[2048,1024]{1,0:T(8,128)(2,1)} %bitcast.51), kind=kOutput, calls=%fused_computation.96 | convolution fusion | flops 2684354560 | bytes 9437184 | tf_op jit(solution)/shard_map/dot_general | solution.py:130
  241.7 0.0 all-gather.10.cloned.1.call-done
  241.7 3.1 %convolution_convert_fusion = bf16[640,2048]{1,0:T(8,128)(2,1)S(1)} fusion(bf16[512,2048]{1,0:T(8,128)(2,1)} %all-gather.10.cloned.1.call-done, f32[640,1024]{1,0:T(8,128)S(1)} %fusion.49), kind=kOutput, calls=%fused_computation.6 | convolution fusion | flops 1345454080 | bytes 7340032 | tf_op jit(solution)/shard_map/dot_general | solution.py:138
  244.9 36.7 %all_to_all.33 = bf16[16,40,2048]{2,1,0:T(8,128)(2,1)S(1)} all-to-all(bf16[16,40,2048]{2,1,0:T(8,128)(2,1)S(1)} %bitcast.53), channel_id=1, replica_groups=mesh['ylo'=2,'core'=2,'z'=4,'x'=4,'yhi'=2] {'z','x'}, dimensions={0} | all-to-all | bytes 5242880 | tf_op jit(solution)/shard_map/all_to_all | solution.py:46
  281.6 0.5 convert_reduce_fusion
  282.1 0.1 multiply_reduce_fusion
  282.2 0.3 copy-done
  282.5 0.0 copy-done.8
  282.5 0.8 add_convert_fusion
  (27 shorter events, 0.4 us)
Async XLA Ops:
  6.5 51.8 %all-gather.6.cloned.1.call-start = ((), (), s32[]{:S(2)}) async-start(), calls=%async_computation.6 | async-start | bytes 2785280 | tf_op jit(solution)/shard_map/all_gather | solution.py:88
  9.2 23.6 %copy-start.9 = (s32[1,8]{1,0:T(1,128)S(1)}, s32[1,8]{1,0:T(1,128)}, u32[]{:S(2)}) copy-start(s32[1,8]{1,0:T(1,128)} %param.14) | copy-start | bytes 100
  9.2 23.8 %copy-start.6 = (f32[16,2048]{1,0:T(8,128)S(1)}, f32[16,2048]{1,0:T(8,128)}, u32[]{:S(2)}) copy-start(f32[16,2048]{1,0:T(8,128)} %param.22) | copy-start | bytes 393220
  26.7 26.1 %all-to-all-start.1 = ((bf16[8,16,16,384]{3,2,1,0:T(8,128)(2,1)}), bf16[8,16,16,384]{3,2,1,0:T(8,128)(2,1)S(1)}, u32[]{:S(2)}, u32[]{:S(2)}) async-start(bf16[8,16,16,384]{3,2,1,0:T(8,128)(2,1)} %stack.10), calls=%async_computation.1 | async-start | bytes 3145728 | tf_op jit(solution)/shard_map/all_to_all | solution.py:16
  31.2 205.0 %all-gather.8.cloned.1.call-start = ((), (), s32[]{:S(2)}) async-start(), calls=%async_computation.7 | async-start | bytes 2785280 | tf_op jit(solution)/shard_map/all_gather | solution.py:131
  85.6 18.4 %collective-permute-start = (bf16[640,256]{0,1:T(8,128)(2,1)S(1)}, bf16[640,256]{0,1:T(8,128)(2,1)S(1)}, u32[]{:S(2)}, u32[]{:S(2)}) collective-permute-start(bf16[640,256]{0,1:T(8,128)(2,1)S(1)} %pad_maximum_fusion.1), channel_id=1, source_target_pairs={{0,1},{1,0},{2,3},{3,2},{4,5},{5,4},{6,7},{7,6},{8,9},{9,8},{10,11... | collective-permute-start | bytes 983048 | tf_op jit(solution)/shard_map/ppermute | solution.py:112
  104.1 1.1 copy-start.1
  149.1 0.9 copy-start.2
  149.2 0.9 copy-start.7
  149.2 1.7 copy-start.3
  149.2 1.8 copy-start.4
  168.5 4.9 %copy-start.5 = (f32[64,2048]{1,0:T(8,128)S(1)}, f32[64,2048]{1,0:T(8,128)}, u32[]{:S(2)}) copy-start(f32[64,2048]{1,0:T(8,128)} %param.25) | copy-start | bytes 1572868
  168.5 62.8 %all-to-all-start.4 = ((bf16[8,16,16,1024]{3,2,1,0:T(8,128)(2,1)}), bf16[8,16,16,1024]{3,2,1,0:T(8,128)(2,1)}, u32[]{:S(2)}, u32[]{:S(2)}) async-start(bf16[8,16,16,1024]{3,2,1,0:T(8,128)(2,1)} %stack.14), calls=%async_computation.4 | async-start | bytes 8388608 | tf_op jit(solution)/shard_map/all_to_all | solution.py:16
  173.1 68.6 %all-gather.10.cloned.1.call-start = ((), (), s32[]{:S(2)}) async-start(), calls=%async_computation.8 | async-start | bytes 2359296 | tf_op jit(solution)/shard_map/all_gather | solution.py:60
  281.6 0.9 copy-start
  281.6 0.9 copy-start.8
Sparse Core Ops, SparseCore 0:
  9.5 48.8 all-gather.5
  151.0 43.2 all-gather.7
  196.0 30.9 all-gather.9
